TPU v7x, 32 devices: a whole 2x2x4 slice. The times are simulated.
32 devices in a mesh: grp: 2 (over y), seq: 4 (over z), ch: 2 (over x), sub: 2 (over core).
Axes of the slice: x: 2, y: 2, z: 4, core: 2. Of those that a mesh axis runs over, the one named last changes fastest.
Arguments:
- token_ids: int32 [2048], P(('grp', 'seq')), parts along dimension 0, may hold values from 0 to 511
- residual_in: bfloat16 [2048, 4096], P(('grp', 'seq'), ('ch', 'sub')), parts along dimension 0, may hold values from -6 to 6
- embedding: bfloat16 [512, 4096], P(None, ('ch', 'sub')), may hold values from -6 to 6
- in_weight: bfloat16 [4096, 3, 2048], P('seq', None, ('ch', 'sub')), may hold values from -0.09375 to 0.09375
- short_filter: float32 [3, 3, 2048], P(None, None, ('ch', 'sub')), may hold values from -3 to 3
- decay_rate: float32 [16, 2048], P(None, ('ch', 'sub')), may hold values from 1e-05 to 0.05
- residue: float32 [16, 2048], P(None, ('ch', 'sub')), may hold values from -0.24 to 0.24
- skip: float32 [2048], P(('ch', 'sub')), may hold values from -4 to 4
Outputs:
- mixed_out: bfloat16 [2048, 2048], P(('grp', 'seq'), ('ch', 'sub')), parts along dimension 0
There are 2 independent parts, one for each index of `grp`. A program takes and returns all parts, laid end to end along the dimension named above; an argument that names none is the same for every part. Nothing has to cross between parts.
All inputs are finite; a program needn't handle non-finite values.
Results may differ from a plain program's by a relative error of at most 0.0095.
Values may be sent and summed in bfloat16 or wider, within the bound.
A program may use at most 64 MiB of HBM per device.

v0:
```python
import functools

import jax
import jax.numpy as jnp
from jax import lax
from jax.experimental import pallas as pl
from jax.experimental.pallas import tpu as pltpu
from jax.sharding import PartitionSpec as P

PRECISE = lax.Precision.HIGHEST
TWO_PI = 6.283185307179586


def shifted(x, axis, by):
    peers = lax.axis_size(axis)
    pairs = [(i, i + by) for i in range(peers) if 0 <= i + by < peers]
    return lax.ppermute(x, axis, pairs)


def swapped(value, axis, apart):
    mask = 2**apart
    pairs = [(source, source ^ mask) for source in range(lax.axis_size(axis))]
    return lax.ppermute(value, axis, pairs)


def reversed_bits(number, bit_count):
    result = jnp.zeros_like(number)
    for section_bit in range(bit_count):
        result = result + (number >> section_bit & 1) * (1 << bit_count - 1 - section_bit)
    return result


def angle_table(left_idx, right_idx, period):
    wrapped = left_idx[:, None] * right_idx[None, :] % period
    return TWO_PI * wrapped.astype(jnp.float32) / period


def complex_mix(mat_re, mat_im, data_re, data_im):
    real_part = jnp.einsum("kr,rjc->kjc", mat_re, data_re, precision=PRECISE) - jnp.einsum(
        "kr,rjc->kjc", mat_im, data_im, precision=PRECISE
    )
    imag_part = jnp.einsum("kr,rjc->kjc", mat_re, data_im, precision=PRECISE) + jnp.einsum(
        "kr,rjc->kjc", mat_im, data_re, precision=PRECISE
    )
    return (real_part, imag_part)


def complex_dot(mat_re, mat_im, data_re, data_im):
    real_part = jnp.dot(mat_re, data_re, precision=PRECISE) - jnp.dot(
        mat_im, data_im, precision=PRECISE
    )
    imag_part = jnp.dot(mat_re, data_im, precision=PRECISE) + jnp.dot(
        mat_im, data_re, precision=PRECISE
    )
    return (real_part, imag_part)


def shards(token_ids, residual_in, embedding, in_weight, short_filter, decay_rate, residue, skip):
    tok_rows = residual_in.shape[0]
    vocab_size = embedding.shape[0]
    channels = skip.shape[0]
    seq_parts = lax.axis_size("seq")
    bit_count = seq_parts.bit_length() - 1
    my_index = lax.axis_index("seq")
    length = tok_rows * seq_parts
    padded_len = 2 * length
    group_rows = tok_rows // seq_parts
    onehot = (token_ids[:, None] == jnp.arange(vocab_size, dtype=jnp.int32)[None, :]).astype(
        jnp.bfloat16
    )
    embedded = jnp.dot(onehot, embedding, preferred_element_type=jnp.float32)
    inputs = (residual_in.astype(jnp.float32) + embedded).astype(jnp.bfloat16)
    features = lax.all_gather(inputs, ("ch", "sub"), axis=1, tiled=True)
    piece_rows = lax.all_gather(in_weight, "seq", axis=0, tiled=True)
    flat_piece = piece_rows.reshape(piece_rows.shape[0], 3 * channels)
    projected = jnp.dot(features, flat_piece, preferred_element_type=jnp.float32)
    projected = projected.astype(jnp.bfloat16).reshape(tok_rows, 3, channels)
    rim_rows = shifted(projected[tok_rows - 2 :], "seq", 1)
    extended = jnp.concatenate([rim_rows, projected], axis=0).astype(jnp.float32)
    mixed_in = (
        short_filter[0] * extended[2:]
        + short_filter[1] * extended[1:-1]
        + short_filter[2] * extended[:-2]
    )
    query_gate = mixed_in[:, 0]
    product = (mixed_in[:, 1] * mixed_in[:, 2]).astype(jnp.bfloat16)
    local_pos = jnp.arange(tok_rows, dtype=jnp.int32)
    sources = jnp.arange(seq_parts, dtype=jnp.int32)
    within_rows = my_index * group_rows + jnp.arange(group_rows, dtype=jnp.int32)
    block_pos = sources[:, None] * tok_rows + within_rows[None, :]
    block_angle = TWO_PI * block_pos.astype(jnp.float32) / padded_len
    pos_angle = TWO_PI * (my_index * tok_rows + local_pos).astype(jnp.float32) / padded_len
    values = product.astype(jnp.float32)
    state_re = jnp.concatenate([values, values * jnp.cos(pos_angle)[:, None]], -1)
    state_im = jnp.concatenate([jnp.zeros_like(values), -values * jnp.sin(pos_angle)[:, None]], -1)
    state_now = jnp.stack([state_re, state_im])
    for section_bit in range(bit_count - 1, -1, -1):
        half_span = 1 << section_bit
        partner = swapped(state_now.astype(jnp.bfloat16), "seq", section_bit).astype(
            state_now.dtype
        )
        upper_half = my_index >> section_bit & 1 == 1
        phase_now = TWO_PI * (my_index % half_span).astype(jnp.float32) / (2 * half_span)
        difference = partner - state_now
        rot_re = difference[0] * jnp.cos(phase_now) + difference[1] * jnp.sin(phase_now)
        rot_im = difference[1] * jnp.cos(phase_now) - difference[0] * jnp.sin(phase_now)
        state_now = jnp.where(upper_half, jnp.stack([rot_re, rot_im]), state_now + partner)
    own_freq = reversed_bits(my_index, bit_count)
    holders = reversed_bits(sources, bit_count)
    twist_angle = TWO_PI * (local_pos * own_freq % length).astype(jnp.float32) / length
    twist_re = jnp.cos(twist_angle)[:, None]
    twist_im = -jnp.sin(twist_angle)[:, None]
    spec_re = state_now[0] * twist_re - state_now[1] * twist_im
    spec_im = state_now[0] * twist_im + state_now[1] * twist_re
    kernel_table = angle_table(local_pos, local_pos, tok_rows)
    dft_re = jnp.cos(kernel_table)
    dft_im = -jnp.sin(kernel_table)
    spec_re, spec_im = complex_dot(dft_re, dft_im, spec_re, spec_im)
    parity = (jnp.arange(2 * channels, dtype=jnp.int32) >= channels).astype(jnp.int32)
    full_freq = 2 * (own_freq + seq_parts * local_pos)[:, None] + parity[None, :]
    freq_angle = TWO_PI * full_freq.astype(jnp.float32) / padded_len
    half_sine = jnp.sin(0.5 * freq_angle)
    sine_full = jnp.sin(freq_angle)
    sign_flip = 1.0 - 2.0 * parity.astype(jnp.float32)
    rates_both = jnp.concatenate([decay_rate, decay_rate], -1)
    residues_both = jnp.concatenate([residue, residue], -1)
    filt_re = jnp.zeros_like(spec_re)
    filt_im = jnp.zeros_like(spec_re)
    for mode_index in range(rates_both.shape[0]):
        rate_now = rates_both[mode_index]
        decay_now = jnp.exp(-rate_now)
        numerator = residues_both[mode_index] * (1.0 - sign_flip * jnp.exp(-rate_now * length))
        denom_re = -jnp.expm1(-rate_now) + 2.0 * decay_now * half_sine * half_sine
        denom_im = decay_now * sine_full
        scaled = numerator / (denom_re * denom_re + denom_im * denom_im)
        filt_re = filt_re + scaled * denom_re
        filt_im = filt_im - scaled * denom_im
    prod_re = spec_re * filt_re - spec_im * filt_im
    prod_im = spec_re * filt_im + spec_im * filt_re
    inv_re, inv_im = complex_dot(dft_re, -dft_im, prod_re, prod_im)
    back_re = inv_re * twist_re + inv_im * twist_im
    back_im = inv_im * twist_re - inv_re * twist_im
    returned = lax.all_to_all(
        jnp.stack([back_re, back_im]).reshape(2, 1, tok_rows, 2 * channels).astype(jnp.bfloat16),
        "seq",
        split_axis=2,
        concat_axis=1,
        tiled=True,
    ).astype(jnp.float32)
    inverse_angle = angle_table(sources, holders, seq_parts)
    block_re, block_im = complex_mix(
        jnp.cos(inverse_angle), jnp.sin(inverse_angle), returned[0], returned[1]
    )
    conv_blocks = (
        block_re[..., :channels]
        + jnp.cos(block_angle)[:, :, None] * block_re[..., channels:]
        - jnp.sin(block_angle)[:, :, None] * block_im[..., channels:]
    )
    conv_blocks = conv_blocks / padded_len
    conv_rows = lax.all_to_all(conv_blocks, "seq", split_axis=0, concat_axis=1, tiled=True)[0]
    mixed_out = (query_gate * (conv_rows + skip * product.astype(jnp.float32))).astype(jnp.bfloat16)
    return mixed_out


def mix_and_scan(rows, modes, part_ref, taps_ref, rate_ref, residue_ref, skip_ref, out_ref, proj, values, gate, result):
    total, lanes = out_ref.shape
    lead = proj.shape[1] - total
    at = pl.ds(pl.multiple_of(lax.axis_index("seq") * lanes, lanes), lanes)
    rates = rate_ref[:, at]
    weights = residue_ref[:, at]
    taps_count = taps_ref.shape[0]
    span = total // rows
    for g in range(3):
        proj[g, :lead, :] = jnp.zeros((lead, lanes), jnp.float32)
    parts = part_ref.shape[0]

    @pl.loop(0, 3)
    def _(g):
        acc = part_ref[0, g].astype(jnp.float32)
        for i in range(1, parts):
            acc = acc + part_ref[i, g].astype(jnp.float32)
        proj[g, lead:, :] = acc.astype(jnp.bfloat16).astype(jnp.float32)

    mixed = []
    for g in range(3):
        acc = None
        for i in range(taps_count):
            term = taps_ref[i, g : g + 1, at] * proj[g, pl.ds(lead - i, total), :]
            acc = term if acc is None else acc + term
        if g == 0:
            gate[...] = acc
        else:
            mixed.append(acc)
    values[...] = (mixed[0] * mixed[1]).astype(jnp.bfloat16).astype(jnp.float32)

    decay = [jnp.broadcast_to(jnp.exp(-rates[m : m + 1, :]), (rows, lanes)) for m in range(modes)]
    zero = jnp.zeros((rows, lanes), jnp.float32)

    def ends(j, state):
        now = values[pl.ds(j, rows, stride=span), :]
        return tuple(u * d + now for u, d in zip(state, decay))

    state = lax.fori_loop(0, span, ends, (zero,) * modes, unroll=4)
    index = lax.broadcasted_iota(jnp.int32, (rows, lanes), 0)

    def down(x, by):
        return jnp.where(index >= by, pltpu.roll(x, by, 0), 0.0)

    entering = []
    for m in range(modes):
        carry = down(state[m], 1)
        by = 1
        while by < rows:
            carry = carry + jnp.exp(-rates[m : m + 1, :] * (span * by)) * down(carry, by)
            by *= 2
        entering.append(carry)
    weight = [jnp.broadcast_to(weights[m : m + 1, :], (rows, lanes)) for m in range(modes)]
    direct = jnp.broadcast_to(skip_ref[:, at], (rows, lanes))

    def scan(j, state):
        here = pl.ds(j, rows, stride=span)
        now = values[here, :]
        state = tuple(u * d + now for u, d in zip(state, decay))
        terms = [u * w for u, w in zip(state, weight)] + [direct * now]
        while len(terms) > 1:
            terms = [a + b for a, b in zip(terms[::2], terms[1::2])] + terms[len(terms) // 2 * 2 :]
        result[here, :] = gate[here, :] * terms[0]
        return state

    lax.fori_loop(0, span, scan, tuple(entering), unroll=4)
    out_ref[...] = result[...].astype(out_ref.dtype)


def convolved(partial, short_filter, decay_rate, residue, skip):
    parts, _, total, lanes = partial.shape
    modes = decay_rate.shape[0]
    rows = 8
    f32 = jnp.float32
    return pl.pallas_call(
        functools.partial(mix_and_scan, rows, modes),
        out_shape=jax.ShapeDtypeStruct((total, lanes), jnp.bfloat16),
        in_specs=[pl.BlockSpec(memory_space=pltpu.VMEM)] * 5,
        out_specs=pl.BlockSpec(memory_space=pltpu.VMEM),
        scratch_shapes=[
            pltpu.VMEM((3, total + 8, lanes), f32),
            pltpu.VMEM((total, lanes), f32),
            pltpu.VMEM((total, lanes), f32),
            pltpu.VMEM((total, lanes), f32),
        ],
        compiler_params=pltpu.CompilerParams(vmem_limit_bytes=40 * 2**20),
    )(partial, short_filter, decay_rate, residue, skip.reshape(1, -1))


MESH = pl.DeviceIdType.MESH


def partial_sums(parts, subs, x_ref, w_ref, out_ref, held, outbox, from_below, from_above, acc, x_send, x_recv, box_send, below_recv, above_recv):
    z = lax.axis_index("seq")
    ch = lax.axis_index("ch")
    sub = lax.axis_index("sub")
    k = ch * subs + sub
    rows = x_ref.shape[0]
    pieces = 8
    half = rows // pieces
    lanes = w_ref.shape[2] // parts
    above = {"seq": lax.rem(z + 1, parts)}
    below = {"seq": lax.rem(z + parts - 1, parts)}
    turned = {"seq": k, "ch": z // subs, "sub": lax.rem(z, subs)}
    mirrored = {"seq": k, "ch": 1 - z // subs, "sub": lax.rem(z, subs)}
    source = {"seq": (1 - ch) * subs + sub, "ch": z // subs, "sub": lax.rem(z, subs)}
    sibling = {"sub": 1 - sub}
    across = {"ch": 1 - ch}
    moves = k != z

    barrier = pltpu.get_barrier_semaphore()

    def greet(device):
        pl.semaphore_signal(barrier, inc=1, device_id=device, device_id_type=MESH)

    greet(sibling)
    greet(across)
    greet(mirrored)
    greet(source)

    @pl.when(moves)
    def _():
        greet(turned)

    @pl.when(z > 0)
    def _():
        greet(below)

    @pl.when(z < parts - 1)
    def _():
        greet(above)

    peers = 4 + moves.astype(jnp.int32) + (z > 0).astype(jnp.int32) + (z < parts - 1).astype(jnp.int32)
    pl.semaphore_wait(barrier, peers)

    def piece(h):
        return pl.ds(h * half, half)

    def copy_x(kind, h, src, slot, device):
        return pltpu.make_async_remote_copy(
            src_ref=src,
            dst_ref=held.at[slot, piece(h)],
            send_sem=x_send.at[kind, h],
            recv_sem=x_recv.at[kind, h],
            device_id=device,
            device_id_type=MESH,
        )

    k_sibling = ch * subs + 1 - sub
    k_across = (1 - ch) * subs + sub
    k_far = (1 - ch) * subs + 1 - sub
    slots = [(k, k_across, k_sibling, k_far), (k_across, k, k_far, k_sibling)]

    @pl.when(moves)
    def _():
        for h in range(0, pieces, 2):
            copy_x(0, h, x_ref.at[piece(h)], z, turned).start()

    @pl.when(jnp.logical_not(moves))
    def _():
        for h in range(0, pieces, 2):
            pltpu.make_async_copy(x_ref.at[piece(h)], held.at[k, piece(h)], x_recv.at[0, h]).start()

    for h in range(1, pieces, 2):
        copy_x(0, h, x_ref.at[piece(h)], z, mirrored).start()

    for h in range(pieces):
        mine = slots[h % 2][0]
        if h % 2:
            copy_x(0, h, x_ref.at[piece(h)], mine, mirrored).wait_recv()
        else:
            @pl.when(moves)
            def _():
                copy_x(0, h, x_ref.at[piece(h)], mine, turned).wait_recv()

            @pl.when(jnp.logical_not(moves))
            def _():
                pltpu.make_async_copy(x_ref.at[piece(h)], held.at[mine, piece(h)], x_recv.at[0, h]).wait()

        copy_x(1, h, held.at[mine, piece(h)], mine, across).start()
        copy_x(2, h, held.at[mine, piece(h)], mine, sibling).start()
    for h in range(pieces):
        other = slots[h % 2][1]
        copy_x(1, h, held.at[other, piece(h)], other, across).wait_recv()
        copy_x(3, h, held.at[other, piece(h)], other, sibling).start()
    def block_at(q):
        return lax.rem(ch + q, 2) * subs + lax.rem(sub + q // 2, 2)

    def own(j, h):
        at = pl.ds(pl.multiple_of(j * lanes, lanes), lanes)
        columns = jnp.concatenate([w_ref[g, :, at] for g in range(3)], axis=1)
        acc[...] = jnp.dot(held[h], columns, preferred_element_type=jnp.float32)

    def rising(j, h):
        return pltpu.make_async_remote_copy(
            src_ref=outbox.at[j, h],
            dst_ref=from_below.at[j, h],
            send_sem=box_send.at[j, h],
            recv_sem=below_recv.at[j, h],
            device_id=above,
            device_id_type=MESH,
        )

    def falling(j, h):
        return pltpu.make_async_remote_copy(
            src_ref=outbox.at[j, h],
            dst_ref=from_above.at[j, h],
            send_sem=box_send.at[j, h],
            recv_sem=above_recv.at[j, h],
            device_id=below,
            device_id_type=MESH,
        )

    def add_below(j, h):
        @pl.when(z > 0)
        def _():
            rising(j, h).wait_recv()
            acc[...] += from_below[j, h].astype(jnp.float32)

    def add_above(j, h):
        @pl.when(z < parts - 1)
        def _():
            falling(j, h).wait_recv()
            acc[...] += from_above[j, h].astype(jnp.float32)

    def step(u, _):
        i = u // parts
        h = block_at(lax.rem(u, parts))
        up = parts - 1 - i

        @pl.when(u == 2)
        def _():
            for n in range(pieces):
                copy_x(2 + n % 2, n, held.at[k, piece(n)], k_sibling, sibling).wait_recv()

        @pl.when(u == 3)
        def _():
            for n in range(pieces):
                copy_x(3 - n % 2, n, held.at[k, piece(n)], k_far, sibling).wait_recv()

        @pl.when(up > z)
        def _():
            own(up, h)
            add_below(up, h)
            outbox[up, h] = acc[...].astype(jnp.bfloat16)
            rising(up, h).start()

        @pl.when(i < z)
        def _():
            own(i, h)
            add_above(i, h)
            outbox[i, h] = acc[...].astype(jnp.bfloat16)
            falling(i, h).start()

        return 0

    lax.fori_loop(0, (parts - 1) * parts, step, 0)

    def last(q, _):
        h = block_at(q)
        own(z, h)
        add_below(z, h)
        add_above(z, h)
        for g in range(3):
            out_ref[0, g, pl.ds(pl.multiple_of(h * rows, rows), rows), :] = acc[:, g * lanes : (g + 1) * lanes].astype(jnp.bfloat16)
        return 0

    lax.fori_loop(0, parts, last, 0)

    def drain(u, _):
        j = u // parts
        h = lax.rem(u, parts)

        @pl.when(j != z)
        def _():
            rising(j, h).wait_send()

        return 0

    lax.fori_loop(0, parts * parts, drain, 0)

    @pl.when(moves)
    def _():
        for h in range(0, pieces, 2):
            copy_x(0, h, x_ref.at[piece(h)], z, turned).wait_send()

    for h in range(1, pieces, 2):
        copy_x(0, h, x_ref.at[piece(h)], z, mirrored).wait_send()
    for h in range(pieces):
        for kind in (1, 2, 3):
            copy_x(kind, h, held.at[k, piece(h)], k, sibling).wait_send()


def summed(inputs, weight, parts, subs):
    rows, width = inputs.shape
    lanes = weight.shape[2] // parts
    box = (parts, parts, rows, 3 * lanes)
    dma = pltpu.SemaphoreType.DMA
    return pl.pallas_call(
        functools.partial(partial_sums, parts, subs),
        out_shape=jax.ShapeDtypeStruct((1, 3, rows * parts, lanes), jnp.bfloat16),
        in_specs=[pl.BlockSpec(memory_space=pltpu.VMEM)] * 2,
        out_specs=pl.BlockSpec(memory_space=pltpu.VMEM),
        scratch_shapes=[
            pltpu.VMEM((parts, rows, width), jnp.bfloat16),
            pltpu.VMEM(box, jnp.bfloat16),
            pltpu.VMEM(box, jnp.bfloat16),
            pltpu.VMEM(box, jnp.bfloat16),
            pltpu.VMEM((rows, 3 * lanes), jnp.float32),
            dma((4, 8)),
            dma((4, 8)),
            dma((parts, parts)),
            dma((parts, parts)),
            dma((parts, parts)),
        ],
        compiler_params=pltpu.CompilerParams(
            collective_id=0, has_side_effects=True, vmem_limit_bytes=48 * 2**20
        ),
    )(inputs, weight)


def fast_shards(token_ids, residual_in, embedding, in_weight, short_filter, decay_rate, residue, skip):
    tok_rows, width = residual_in.shape
    vocab_size = embedding.shape[0]
    channels = skip.shape[0]
    seq_parts = lax.axis_size("seq")
    onehot = (token_ids[:, None] == jnp.arange(vocab_size, dtype=jnp.int32)[None, :]).astype(jnp.bfloat16)
    embedded = jnp.dot(onehot, embedding, preferred_element_type=jnp.float32)
    inputs = (residual_in.astype(jnp.float32) + embedded).astype(jnp.bfloat16)
    weight = in_weight.transpose(1, 0, 2)
    partial = summed(inputs, weight, seq_parts, lax.axis_size("sub"))

    mixed = convolved(partial, short_filter, decay_rate, residue, skip)
    return lax.all_to_all(mixed, "seq", split_axis=0, concat_axis=1, tiled=True)


def fits(mesh):
    seq_parts = mesh.shape["seq"]
    return mesh.shape["ch"] == 2 and mesh.shape["sub"] == 2 and seq_parts == mesh.shape["ch"] * mesh.shape["sub"]


def solution(mesh):
    return jax.shard_map(
        fast_shards if fits(mesh) else shards,
        mesh=mesh,
        in_specs=(
            P(("grp", "seq")),
            P(("grp", "seq"), ("ch", "sub")),
            P(None, ("ch", "sub")),
            P("seq", None, ("ch", "sub")),
            P(None, None, ("ch", "sub")),
            P(None, ("ch", "sub")),
            P(None, ("ch", "sub")),
            P(("ch", "sub")),
        ),
        out_specs=P(("grp", "seq"), ("ch", "sub")),
        check_vma=False,
    )
```

profile of v0, /device:TPU:6, one launch (start us, length us, event | category | flops | bytes accessed | tf_op | source)
XLA Modules:
  0.0 116.2 jit_solution(2400003824295741581)
XLA Ops:
  0.0 0.0 copy-start
  0.0 0.0 copy-start.5
  0.0 0.0 copy-start.3
  0.0 0.0 copy-start.2
  0.0 1.2 %copy-done = bf16[512,1024]{1,0:T(8,128)(2,1)S(1)} copy-done((bf16[512,1024]{1,0:T(8,128)(2,1)S(1)}, bf16[512,1024]{1,0:T(8,128)(2,1)}, u32[]{:S(2)}) %copy-start) | copy-done | bytes 1048600
  1.2 0.0 copy-start.4
  1.2 1.5 %fusion.x_ref = bf16[256,1024]{1,0:T(8,128)(2,1)S(1)} fusion(bf16[512,1024]{1,0:T(8,128)(2,1)S(1)} %copy-done, bf16[256,1024]{1,0:T(8,128)(2,1)} %param.9, s32[256]{0:T(256)} %param.8), kind=kOutput, calls=%fused_computation.1 | convolution fusion | flops 269352960 | bytes 2098176 | tf_op jit(solution)/shard_map/dot_general | solution.py:492
  2.8 0.0 copy-start.1
  2.8 1.9 %copy-done.1 = bf16[1024,3,512]{2,0,1:T(8,128)(2,1)S(1)} copy-done((bf16[1024,3,512]{2,0,1:T(8,128)(2,1)S(1)}, bf16[1024,3,512]{2,0,1:T(8,128)(2,1)}, u32[]{:S(2)}) %copy-start.1) | copy-done | bytes 3145752
  4.7 88.7 %shard_map.82.part_ref = bf16[1,3,1024,128]{3,2,1,0:T(8,128)(2,1)S(1)} custom-call(bf16[256,1024]{1,0:T(8,128)(2,1)S(1)} %fusion.x_ref, bf16[3,1024,512]{2,1,0:T(8,128)(2,1)S(1)} %bitcast.10), custom_call_target="tpu_custom_call" | custom-call | tf_op jit(solution)/shard_map/pallas_call | solution.py:463
  93.4 0.0 copy-done.5
  93.4 0.0 copy-done.3
  93.4 0.0 copy-done.2
  93.4 0.0 copy-done.4
  93.4 3.4 %shard_map.83 = bf16[1024,128]{1,0:T(8,128)(2,1)S(1)} custom-call(bf16[1,3,1024,128]{3,2,1,0:T(8,128)(2,1)S(1)} %shard_map.82.part_ref, f32[3,3,512]{2,1,0:T(4,128)S(1)} %copy-done.4, f32[16,512]{1,0:T(8,128)S(1)} %copy-done.2, f32[16,512]{1,0:T(8,128)S(1)} %copy-done.3, f32[1,512]{1,0:T(1,128)S(1)} %bitcast.12), custom_call_target="tpu_custom_call" | custom-call | tf_op jit(solution)/shard_map/pallas_call | solution.py:239
  96.8 18.7 %all_to_all.19 = bf16[4,256,128]{2,1,0:T(8,128)(2,1)S(1)} all-to-all(bf16[4,256,128]{2,1,0:T(8,128)(2,1)S(1)} %bitcast.11), channel_id=1, replica_groups=mesh['grp'=2,'seq'=4,'ch'=2,'sub'=2] {'seq'}, dimensions={0} | all-to-all | bytes 524288 | tf_op jit(solution)/shard_map/all_to_all | solution.py:498
  115.5 0.7 copy_bitcast_fusion
Async XLA Ops:
  0.0 1.2 %copy-start = (bf16[512,1024]{1,0:T(8,128)(2,1)S(1)}, bf16[512,1024]{1,0:T(8,128)(2,1)}, u32[]{:S(2)}) copy-start(bf16[512,1024]{1,0:T(8,128)(2,1)} %param.10) | copy-start | bytes 3145732
  0.0 93.4 %copy-start.5 = (f32[512]{0:T(512)S(1)}, f32[512]{0:T(512)}, u32[]{:S(2)}) copy-start(f32[512]{0:T(512)} %param.15) | copy-start | bytes 6148
  0.0 93.4 %copy-start.3 = (f32[16,512]{1,0:T(8,128)S(1)}, f32[16,512]{1,0:T(8,128)}, u32[]{:S(2)}) copy-start(f32[16,512]{1,0:T(8,128)} %residue_ref.1) | copy-start | bytes 98308
  0.0 93.4 %copy-start.2 = (f32[16,512]{1,0:T(8,128)S(1)}, f32[16,512]{1,0:T(8,128)}, u32[]{:S(2)}) copy-start(f32[16,512]{1,0:T(8,128)} %rate_ref.1) | copy-start | bytes 98308
  1.2 92.2 %copy-start.4 = (f32[3,3,512]{2,1,0:T(4,128)S(1)}, f32[3,3,512]{2,1,0:T(4,128)}, u32[]{:S(2)}) copy-start(f32[3,3,512]{2,1,0:T(4,128)} %taps_ref.1) | copy-start | bytes 55300
  2.8 1.9 %copy-start.1 = (bf16[1024,3,512]{2,0,1:T(8,128)(2,1)S(1)}, bf16[1024,3,512]{2,0,1:T(8,128)(2,1)}, u32[]{:S(2)}) copy-start(bf16[1024,3,512]{2,0,1:T(8,128)(2,1)} %param.11) | copy-start | bytes 9437188
where the time goes:
time: 116 us
  Pallas kernels  92.1 us (79%)
  blocking collectives  18.7 us (16%)
  local copies, waits for them, and re-layouts  3.84 us (3%)
  matrix products  1.55 us (1%)
    pallas_call x1, Pallas kernels, summed(): pl.pallas_call(functools.partial(partial_sums, parts, subs), out_shape=ja...  88.7 us
    all_to_all x1, blocking collectives, fast_shards(): return lax.all_to_all(mixed, 'seq', split_axis=0, concat_axis=1, tiled=True)  18.7 us
    pallas_call x1, Pallas kernels, convolved(): pl.pallas_call(functools.partial(mix_and_scan, rows, modes), out_shape=ja...  3.39 us
    unnamed x12, local copies, waits for them, and re-layouts  3.11 us

commit v1 on v0

v1 whole, which is shorter than its diff:
```python
import functools

import jax
import jax.numpy as jnp
from jax import lax
from jax.experimental import pallas as pl
from jax.experimental.pallas import tpu as pltpu
from jax.sharding import PartitionSpec as P

PRECISE = lax.Precision.HIGHEST
TWO_PI = 6.283185307179586


def shifted(x, axis, by):
    peers = lax.axis_size(axis)
    pairs = [(i, i + by) for i in range(peers) if 0 <= i + by < peers]
    return lax.ppermute(x, axis, pairs)


def swapped(value, axis, apart):
    mask = 2**apart
    pairs = [(source, source ^ mask) for source in range(lax.axis_size(axis))]
    return lax.ppermute(value, axis, pairs)


def reversed_bits(number, bit_count):
    result = jnp.zeros_like(number)
    for section_bit in range(bit_count):
        result = result + (number >> section_bit & 1) * (1 << bit_count - 1 - section_bit)
    return result


def angle_table(left_idx, right_idx, period):
    wrapped = left_idx[:, None] * right_idx[None, :] % period
    return TWO_PI * wrapped.astype(jnp.float32) / period


def complex_mix(mat_re, mat_im, data_re, data_im):
    real_part = jnp.einsum("kr,rjc->kjc", mat_re, data_re, precision=PRECISE) - jnp.einsum(
        "kr,rjc->kjc", mat_im, data_im, precision=PRECISE
    )
    imag_part = jnp.einsum("kr,rjc->kjc", mat_re, data_im, precision=PRECISE) + jnp.einsum(
        "kr,rjc->kjc", mat_im, data_re, precision=PRECISE
    )
    return (real_part, imag_part)


def complex_dot(mat_re, mat_im, data_re, data_im):
    real_part = jnp.dot(mat_re, data_re, precision=PRECISE) - jnp.dot(
        mat_im, data_im, precision=PRECISE
    )
    imag_part = jnp.dot(mat_re, data_im, precision=PRECISE) + jnp.dot(
        mat_im, data_re, precision=PRECISE
    )
    return (real_part, imag_part)


def shards(token_ids, residual_in, embedding, in_weight, short_filter, decay_rate, residue, skip):
    tok_rows = residual_in.shape[0]
    vocab_size = embedding.shape[0]
    channels = skip.shape[0]
    seq_parts = lax.axis_size("seq")
    bit_count = seq_parts.bit_length() - 1
    my_index = lax.axis_index("seq")
    length = tok_rows * seq_parts
    padded_len = 2 * length
    group_rows = tok_rows // seq_parts
    onehot = (token_ids[:, None] == jnp.arange(vocab_size, dtype=jnp.int32)[None, :]).astype(
        jnp.bfloat16
    )
    embedded = jnp.dot(onehot, embedding, preferred_element_type=jnp.float32)
    inputs = (residual_in.astype(jnp.float32) + embedded).astype(jnp.bfloat16)
    features = lax.all_gather(inputs, ("ch", "sub"), axis=1, tiled=True)
    piece_rows = lax.all_gather(in_weight, "seq", axis=0, tiled=True)
    flat_piece = piece_rows.reshape(piece_rows.shape[0], 3 * channels)
    projected = jnp.dot(features, flat_piece, preferred_element_type=jnp.float32)
    projected = projected.astype(jnp.bfloat16).reshape(tok_rows, 3, channels)
    rim_rows = shifted(projected[tok_rows - 2 :], "seq", 1)
    extended = jnp.concatenate([rim_rows, projected], axis=0).astype(jnp.float32)
    mixed_in = (
        short_filter[0] * extended[2:]
        + short_filter[1] * extended[1:-1]
        + short_filter[2] * extended[:-2]
    )
    query_gate = mixed_in[:, 0]
    product = (mixed_in[:, 1] * mixed_in[:, 2]).astype(jnp.bfloat16)
    local_pos = jnp.arange(tok_rows, dtype=jnp.int32)
    sources = jnp.arange(seq_parts, dtype=jnp.int32)
    within_rows = my_index * group_rows + jnp.arange(group_rows, dtype=jnp.int32)
    block_pos = sources[:, None] * tok_rows + within_rows[None, :]
    block_angle = TWO_PI * block_pos.astype(jnp.float32) / padded_len
    pos_angle = TWO_PI * (my_index * tok_rows + local_pos).astype(jnp.float32) / padded_len
    values = product.astype(jnp.float32)
    state_re = jnp.concatenate([values, values * jnp.cos(pos_angle)[:, None]], -1)
    state_im = jnp.concatenate([jnp.zeros_like(values), -values * jnp.sin(pos_angle)[:, None]], -1)
    state_now = jnp.stack([state_re, state_im])
    for section_bit in range(bit_count - 1, -1, -1):
        half_span = 1 << section_bit
        partner = swapped(state_now.astype(jnp.bfloat16), "seq", section_bit).astype(
            state_now.dtype
        )
        upper_half = my_index >> section_bit & 1 == 1
        phase_now = TWO_PI * (my_index % half_span).astype(jnp.float32) / (2 * half_span)
        difference = partner - state_now
        rot_re = difference[0] * jnp.cos(phase_now) + difference[1] * jnp.sin(phase_now)
        rot_im = difference[1] * jnp.cos(phase_now) - difference[0] * jnp.sin(phase_now)
        state_now = jnp.where(upper_half, jnp.stack([rot_re, rot_im]), state_now + partner)
    own_freq = reversed_bits(my_index, bit_count)
    holders = reversed_bits(sources, bit_count)
    twist_angle = TWO_PI * (local_pos * own_freq % length).astype(jnp.float32) / length
    twist_re = jnp.cos(twist_angle)[:, None]
    twist_im = -jnp.sin(twist_angle)[:, None]
    spec_re = state_now[0] * twist_re - state_now[1] * twist_im
    spec_im = state_now[0] * twist_im + state_now[1] * twist_re
    kernel_table = angle_table(local_pos, local_pos, tok_rows)
    dft_re = jnp.cos(kernel_table)
    dft_im = -jnp.sin(kernel_table)
    spec_re, spec_im = complex_dot(dft_re, dft_im, spec_re, spec_im)
    parity = (jnp.arange(2 * channels, dtype=jnp.int32) >= channels).astype(jnp.int32)
    full_freq = 2 * (own_freq + seq_parts * local_pos)[:, None] + parity[None, :]
    freq_angle = TWO_PI * full_freq.astype(jnp.float32) / padded_len
    half_sine = jnp.sin(0.5 * freq_angle)
    sine_full = jnp.sin(freq_angle)
    sign_flip = 1.0 - 2.0 * parity.astype(jnp.float32)
    rates_both = jnp.concatenate([decay_rate, decay_rate], -1)
    residues_both = jnp.concatenate([residue, residue], -1)
    filt_re = jnp.zeros_like(spec_re)
    filt_im = jnp.zeros_like(spec_re)
    for mode_index in range(rates_both.shape[0]):
        rate_now = rates_both[mode_index]
        decay_now = jnp.exp(-rate_now)
        numerator = residues_both[mode_index] * (1.0 - sign_flip * jnp.exp(-rate_now * length))
        denom_re = -jnp.expm1(-rate_now) + 2.0 * decay_now * half_sine * half_sine
        denom_im = decay_now * sine_full
        scaled = numerator / (denom_re * denom_re + denom_im * denom_im)
        filt_re = filt_re + scaled * denom_re
        filt_im = filt_im - scaled * denom_im
    prod_re = spec_re * filt_re - spec_im * filt_im
    prod_im = spec_re * filt_im + spec_im * filt_re
    inv_re, inv_im = complex_dot(dft_re, -dft_im, prod_re, prod_im)
    back_re = inv_re * twist_re + inv_im * twist_im
    back_im = inv_im * twist_re - inv_re * twist_im
    returned = lax.all_to_all(
        jnp.stack([back_re, back_im]).reshape(2, 1, tok_rows, 2 * channels).astype(jnp.bfloat16),
        "seq",
        split_axis=2,
        concat_axis=1,
        tiled=True,
    ).astype(jnp.float32)
    inverse_angle = angle_table(sources, holders, seq_parts)
    block_re, block_im = complex_mix(
        jnp.cos(inverse_angle), jnp.sin(inverse_angle), returned[0], returned[1]
    )
    conv_blocks = (
        block_re[..., :channels]
        + jnp.cos(block_angle)[:, :, None] * block_re[..., channels:]
        - jnp.sin(block_angle)[:, :, None] * block_im[..., channels:]
    )
    conv_blocks = conv_blocks / padded_len
    conv_rows = lax.all_to_all(conv_blocks, "seq", split_axis=0, concat_axis=1, tiled=True)[0]
    mixed_out = (query_gate * (conv_rows + skip * product.astype(jnp.float32))).astype(jnp.bfloat16)
    return mixed_out


MESH = pl.DeviceIdType.MESH
PIECES = 4
AHEAD = 3
SEGMENTS = 8


def fused_block(
    x_ref, w_ref, taps_ref, rate_ref, residue_ref, skip_ref, out_ref,
    held, weights, stage, outbox, inbox, edge, halo, proj, values, conv, enter, ends, states,
    load_sem, wide_send, wide_recv, weight_send, weight_recv, x_send, x_recv, via_send, via_recv,
    box_send, box_recv, edge_send, edge_recv, end_send, end_recv,
):
    y = lax.axis_index("grp")
    z = lax.axis_index("seq")
    ch = lax.axis_index("ch")
    sub = lax.axis_index("sub")
    rows = x_ref.shape[0]
    width = x_ref.shape[1]
    parts, tall = 4, width // 2
    units, lanes = weights.shape[1], weights.shape[3]
    blocks = units // 3
    pairs = 2 * blocks
    modes = rate_ref.shape[0]
    taps_count = taps_ref.shape[0]
    span = rows // SEGMENTS
    f32, bf16 = jnp.float32, jnp.bfloat16

    side = z // 2
    near = 1 + side
    outer = 3 * side
    far_near = 2 - side
    far_outer = 3 - outer
    is_outer = z == outer
    is_inner = z == near
    mine = lax.rem(z, 2)
    across = {"ch": 1 - ch}
    sibling = {"sub": 1 - sub}
    other_group = {"grp": 1 - y}

    def remote(src, dst, send, recv, device):
        return pltpu.make_async_remote_copy(
            src_ref=src, dst_ref=dst, send_sem=send, recv_sem=recv, device_id=device, device_id_type=MESH
        )

    def place(u):
        pair = u < pairs
        return jnp.where(pair, 1 + lax.rem(u, 2), 0), jnp.where(pair, u // 2, u - pairs)

    def load(u):
        g, h = (1 + u % 2, u // 2) if u < pairs else (0, u - pairs)
        return pltpu.make_async_copy(
            w_ref.at[g, :, pl.ds(h * lanes, lanes)], weights.at[mine, u], load_sem.at[u]
        )

    def loaded(u):
        pltpu.make_async_copy(w_ref.at[0, :, pl.ds(0, lanes)], weights.at[mine, u], load_sem.at[u]).wait()

    for u in range(units):
        load(u).start()
    halo[...] = jnp.zeros_like(halo)
    states[...] = jnp.zeros_like(states)

    barrier = pltpu.get_barrier_semaphore()
    for device in (across, sibling, other_group):
        pl.semaphore_signal(barrier, inc=1, device_id=device, device_id_type=MESH)
    for apart in range(1, parts):
        pl.semaphore_signal(barrier, inc=1, device_id={"seq": lax.rem(z + apart, parts)}, device_id_type=MESH)
    pl.semaphore_wait(barrier, 3 + parts - 1)

    share = pl.ds(pl.multiple_of(y * tall, tall), tall)

    def weight_up(u):
        at = weights.at[mine, u, share]
        return remote(at, at, weight_send.at[u], weight_recv.at[u], {"seq": near})

    def weight_wide(u):
        at = weights.at[1 - mine, u, share]
        return remote(at, at, wide_send.at[u], wide_recv.at[u], other_group)

    def weight_share(u):
        at = weights.at[1 - mine, u, share]
        remote(at, at, weight_send.at[u], weight_recv.at[u], other_group).wait_recv()
        weight_wide(u).start()

    step = rows // PIECES
    direct = PIECES // 2

    def piece(p):
        return pl.ds(p * step, step) if isinstance(p, int) else pl.ds(pl.multiple_of(p * step, step), step)

    def target(c):
        f = 2 * c + sub
        return jnp.where((f == z) & is_outer, z, 1 + c)

    goal = target(ch)
    relay_goal = target(1 - ch)
    stays = goal == z
    relay_stays = relay_goal == z

    def own_direct(p):
        return remote(x_ref.at[piece(p)], held.at[z, sub, piece(p)], x_send.at[0, p], x_recv.at[z, sub, p], {"seq": goal})

    def own_local(p):
        return pltpu.make_async_copy(x_ref.at[piece(p)], held.at[z, sub, piece(p)], x_recv.at[z, sub, p])

    def own_across(p):
        return remote(x_ref.at[piece(p)], held.at[z, sub, piece(p)], x_send.at[0, p], x_recv.at[z, sub, p], across)

    def own_via(p):
        return remote(x_ref.at[piece(p)], stage.at[p - direct], x_send.at[0, p], via_recv.at[p - direct], across)

    def relay(p):
        return remote(
            stage.at[p - direct], held.at[z, sub, piece(p)], via_send.at[p - direct], x_recv.at[z, sub, p],
            {"seq": relay_goal},
        )

    def send_via():
        @pl.when(stays)
        def _():
            for p in range(direct, PIECES):
                own_across(p).start()

        @pl.when(jnp.logical_not(stays))
        def _():
            for p in range(direct, PIECES):
                own_via(p).start()

    def send_direct():
        @pl.when(stays)
        def _():
            for p in range(direct):
                own_local(p).start()

        @pl.when(jnp.logical_not(stays))
        def _():
            for p in range(direct):
                own_direct(p).start()

    def send_relay():
        @pl.when(jnp.logical_not(relay_stays))
        def _():
            for p in range(direct, PIECES):
                own_via(p).wait_recv()
                relay(p).start()

    at_home = ch == side
    first = jnp.where(at_home, 0, direct)
    second = direct - first

    def arrived(t, s, p):
        at = held.at[t, s, piece(p)]
        remote(at, at, x_send.at[1, p], x_recv.at[t, s, p], across).wait_recv()

    def to_across(t, p):
        at = held.at[t, sub, piece(p)]
        return remote(at, at, x_send.at[1 + t, p], x_recv.at[t, sub, p], across)

    def to_sibling(t, p):
        at = held.at[t, sub, piece(p)]
        return remote(at, at, x_send.at[1 + parts + t, p], x_recv.at[t, sub, p], sibling)

    def primary(t):
        for n in range(direct):
            p = first + n
            arrived(t, sub, p)
            to_across(t, p).start()
            to_sibling(t, p).start()

    def secondary(t):
        for n in range(PIECES - direct):
            p = second + n
            arrived(t, sub, p)
            to_sibling(t, p).start()

    def from_sibling(t):
        for p in range(PIECES):
            arrived(t, 1 - sub, p)

    def outgoing(kind, u, device, there):
        return remote(
            outbox.at[kind, u], inbox.at[there, u], box_send.at[kind, u], box_recv.at[there, u], device
        )

    def both(t, u):
        return jnp.dot(held[t, 0], weights[0, u], preferred_element_type=f32) + jnp.dot(
            held[t, 1], weights[1, u], preferred_element_type=f32
        )

    def one(t, u):
        return jnp.dot(held[t, mine], weights[mine, u], preferred_element_type=f32)

    def received(kind, u):
        outgoing(kind, u, across, kind).wait_recv()
        return inbox[kind, u].astype(f32)

    def far(kind, t, u):
        outbox[kind, u] = both(t, u).astype(bf16)
        outgoing(kind, u, {"seq": far_near}, kind).start()

    def weights_ready(u):
        loaded(u)
        at = weights.at[1 - mine, u, share]
        remote(at, at, wide_send.at[u], wide_recv.at[u], other_group).wait_recv()

    def to_outer(u):
        acc = one(outer, u)
        outbox[2, u] = (acc + received(1, u)).astype(bf16)
        outgoing(2, u, {"seq": outer}, 0).start()

    def edge_copy(u):
        return remote(edge.at[u], halo.at[u], edge_send.at[u], edge_recv.at[u], {"seq": z + 1})

    def finished(acc, u):
        total = (acc + received(0, u)).astype(bf16)
        proj[u, SEGMENTS:, :] = total.astype(f32)

        @pl.when(z < parts - 1)
        def _():
            edge[u] = total[rows - 16 :]
            edge_copy(u).start()

    def lanes_at(h):
        return pl.ds(pl.multiple_of(h * lanes, lanes), lanes)

    def mixed(g, u, h):
        proj[u, :SEGMENTS, :] = halo[u].astype(f32)[16 - SEGMENTS :]
        acc = None
        for i in range(taps_count):
            term = taps_ref[i, g : g + 1, lanes_at(h)] * proj[u, pl.ds(SEGMENTS - i, rows), :]
            acc = term if acc is None else acc + term
        return acc

    def halo_ready(u):
        @pl.when(z > 0)
        def _():
            remote(edge.at[u], halo.at[u], edge_send.at[u], edge_recv.at[u], across).wait_recv()

    index = lax.broadcasted_iota(jnp.int32, (SEGMENTS, lanes), 0)

    def wide(row):
        return jnp.broadcast_to(row, (SEGMENTS, lanes))

    def end_copy(h, apart):
        return remote(
            ends.at[h], states.at[z, h], end_send.at[apart - 1, h], end_recv.at[z, h], {"seq": z + apart}
        )

    def local_scan(h):
        rates = rate_ref[:, lanes_at(h)]
        decay = [wide(jnp.exp(-rates[m : m + 1, :])) for m in range(modes)]
        zero = jnp.zeros((SEGMENTS, lanes), f32)

        def advance(j, state):
            now = values[h, pl.ds(j, SEGMENTS, stride=span), :]
            return tuple(v * d + now for v, d in zip(state, decay))

        state = lax.fori_loop(0, span, advance, (zero,) * modes, unroll=4)

        def down(v, by):
            return jnp.where(index >= by, pltpu.roll(v, by, 0), 0.0)

        for m in range(modes):
            carry = down(state[m], 1)
            by = 1
            while by < SEGMENTS:
                carry = carry + jnp.exp(-rates[m : m + 1, :] * (span * by)) * down(carry, by)
                by *= 2
            enter[h, m] = carry
            last = slice(SEGMENTS - 1, SEGMENTS)
            ends[h, m : m + 1, :] = jnp.exp(-rates[m : m + 1, :] * span) * carry[last] + state[m][last]
        for apart in range(1, parts):
            @pl.when(z + apart < parts)
            def _():
                end_copy(h, apart).start()

    def full_scan(h):
        rates = rate_ref[:, lanes_at(h)]
        scale = residue_ref[:, lanes_at(h)]
        for t in range(parts - 1):
            @pl.when(t < z)
            def _():
                remote(ends.at[h], states.at[t, h], end_send.at[0, h], end_recv.at[t, h], across).wait_recv()

        decay = [wide(jnp.exp(-rates[m : m + 1, :])) for m in range(modes)]
        weight = [wide(scale[m : m + 1, :]) for m in range(modes)]
        whole = jnp.exp(-rates * rows)
        start = states[0, h]
        for t in range(1, parts - 1):
            start = jnp.where(t < z, start * whole + states[t, h], start)
        steps = (index * span).astype(f32)
        begin = tuple(
            enter[h, m] + jnp.exp(-rates[m : m + 1, :] * steps) * start[m : m + 1, :] for m in range(modes)
        )
        skips = wide(skip_ref[:, lanes_at(h)])

        def advance(j, state):
            here = pl.ds(j, SEGMENTS, stride=span)
            now = values[h, here, :]
            state = tuple(v * d + now for v, d in zip(state, decay))
            terms = [v * w for v, w in zip(state, weight)] + [skips * now]
            while len(terms) > 1:
                terms = [a + b for a, b in zip(terms[::2], terms[1::2])] + terms[len(terms) // 2 * 2 :]
            conv[h, here, :] = terms[0]
            return state

        lax.fori_loop(0, span, advance, begin, unroll=4)

    def mix(u):
        halo_ready(u)
        _, h = place(u)

        @pl.when((u < pairs) & (lax.rem(u, 2) == 1))
        def _():
            product = mixed(1, u - 1, h) * mixed(2, u, h)
            values[h] = product.astype(bf16).astype(f32)
            local_scan(h)

        @pl.when(u >= pairs)
        def _():
            out_ref[:, lanes_at(h)] = (mixed(0, u, h) * conv[h]).astype(out_ref.dtype)

    @pl.when(is_outer)
    def _():
        loaded(0)
        weight_up(0).start()
        send_via()
        send_direct()
        for u in range(1, AHEAD):
            loaded(u)
            weight_up(u).start()
        send_relay()
        for u in range(AHEAD, units):
            loaded(u)
            weight_up(u).start()

        @pl.when(sub == mine)
        def _():
            primary(z)
            secondary(z)

        @pl.when(sub != mine)
        def _():
            from_sibling(z)

        @pl.loop(0, units + 1)
        def _(u):
            @pl.when(u > pairs)
            def _():
                full_scan(u - 1 - pairs)

            @pl.when(u < units)
            def _():
                finished(one(z, u), u)

            @pl.when(u > 0)
            def _():
                mix(u - 1)

    @pl.when(is_inner)
    def _():
        handles_near = sub == mine
        send_via()
        send_direct()
        send_relay()
        weight_share(0)
        primary(far_near)
        weight_share(1)
        secondary(far_near)
        primary(far_outer)
        for u in range(2, AHEAD):
            weight_share(u)
        from_sibling(far_near)

        @pl.loop(0, AHEAD)
        def _(u):
            weights_ready(u)
            far(0, far_near, u)

        secondary(far_outer)
        primary(z)
        weight_share(AHEAD)

        @pl.when(handles_near)
        def _():
            primary(outer)

        from_sibling(far_outer)
        lag = 3

        @pl.loop(0, units + lag)
        def _(i):
            @pl.when(i < units)
            def _():
                far(1, far_outer, i)

            @pl.when(i + AHEAD < units)
            def _():
                weights_ready(i + AHEAD)
                far(0, far_near, i + AHEAD)

            @pl.when(i + AHEAD + 1 < units)
            def _():
                weight_share(i + AHEAD + 1)

            @pl.when(i == 0)
            def _():
                secondary(z)

                @pl.when(handles_near)
                def _():
                    secondary(outer)

                from_sibling(z)

                @pl.when(jnp.logical_not(handles_near))
                def _():
                    from_sibling(outer)

            @pl.when((i > 0) & (i <= units))
            def _():
                to_outer(i - 1)
                finished(both(z, i - 1), i - 1)

            @pl.when((i >= pairs + lag - 1) & (i < units + lag - 1))
            def _():
                full_scan(i - pairs - lag + 1)

            @pl.when(i >= lag)
            def _():
                mix(i - lag)

    for p in range(PIECES):
        @pl.when(jnp.logical_not(stays) | (p >= direct))
        def _():
            own_direct(p).wait_send()

    @pl.when(jnp.logical_not(relay_stays))
    def _():
        for p in range(direct, PIECES):
            relay(p).wait_send()

    def sent(t):
        for n in range(direct):
            to_across(t, first + n).wait_send()
        for p in range(PIECES):
            to_sibling(t, p).wait_send()

    @pl.when(is_outer & (sub == mine))
    def _():
        sent(z)

    @pl.when(is_inner)
    def _():
        sent(far_near)
        sent(far_outer)
        sent(z)

        @pl.when(sub == mine)
        def _():
            sent(outer)

    @pl.loop(0, units)
    def _(u):
        @pl.when(is_outer)
        def _():
            weight_up(u).wait_send()

        @pl.when(is_inner)
        def _():
            weight_wide(u).wait_send()
            for kind in range(3):
                outgoing(kind, u, across, 0).wait_send()

        @pl.when(z < parts - 1)
        def _():
            remote(edge.at[u], halo.at[u], edge_send.at[u], edge_recv.at[u], across).wait_send()

    for h in range(blocks):
        for apart in range(1, parts):
            @pl.when(z + apart < parts)
            def _():
                remote(
                    ends.at[h], states.at[0, h], end_send.at[apart - 1, h], end_recv.at[0, h], across
                ).wait_send()


def fused(inputs, weight, short_filter, decay_rate, residue, skip):
    rows, width = inputs.shape
    groups, _, channels = weight.shape
    parts = 4
    modes = decay_rate.shape[0]
    lanes = 128
    blocks = channels // lanes
    units = groups * blocks
    dma = pltpu.SemaphoreType.DMA
    f32, bf16 = jnp.float32, jnp.bfloat16
    vmem = pl.BlockSpec(memory_space=pltpu.VMEM)
    return pl.pallas_call(
        fused_block,
        out_shape=jax.ShapeDtypeStruct((rows, channels), jnp.bfloat16),
        in_specs=[vmem, pl.BlockSpec(memory_space=pl.ANY)] + [vmem] * 4,
        out_specs=vmem,
        scratch_shapes=[
            pltpu.VMEM((parts, 2, rows, width), bf16),
            pltpu.VMEM((2, units, width, lanes), bf16),
            pltpu.VMEM((PIECES - PIECES // 2, rows // PIECES, width), bf16),
            pltpu.VMEM((3, units, rows, lanes), bf16),
            pltpu.VMEM((2, units, rows, lanes), bf16),
            pltpu.VMEM((units, 16, lanes), bf16),
            pltpu.VMEM((units, 16, lanes), bf16),
            pltpu.VMEM((units, rows + SEGMENTS, lanes), f32),
            pltpu.VMEM((blocks, rows, lanes), f32),
            pltpu.VMEM((blocks, rows, lanes), f32),
            pltpu.VMEM((blocks, modes, SEGMENTS, lanes), f32),
            pltpu.VMEM((blocks, modes, lanes), f32),
            pltpu.VMEM((parts - 1, blocks, modes, lanes), f32),
            dma((units,)),
            dma((units,)),
            dma((units,)),
            dma((units,)),
            dma((units,)),
            dma((1 + 2 * parts, PIECES)),
            dma((parts, 2, PIECES)),
            dma((PIECES - PIECES // 2,)),
            dma((PIECES - PIECES // 2,)),
            dma((3, units)),
            dma((2, units)),
            dma((units,)),
            dma((units,)),
            dma((parts - 1, blocks)),
            dma((parts - 1, blocks)),
        ],
        compiler_params=pltpu.CompilerParams(
            collective_id=0, has_side_effects=True, vmem_limit_bytes=60 * 2**20
        ),
    )(inputs, weight, short_filter, decay_rate, residue, skip.reshape(1, -1))


def fast_shards(token_ids, residual_in, embedding, in_weight, short_filter, decay_rate, residue, skip):
    vocab_size = embedding.shape[0]
    onehot = (token_ids[:, None] == jnp.arange(vocab_size, dtype=jnp.int32)[None, :]).astype(jnp.bfloat16)
    embedded = jnp.dot(onehot, embedding, preferred_element_type=jnp.float32)
    inputs = (residual_in.astype(jnp.float32) + embedded).astype(jnp.bfloat16)
    return fused(inputs, in_weight.transpose(1, 0, 2), short_filter, decay_rate, residue, skip)


def fits(mesh):
    shape = mesh.shape
    return shape["seq"] == 4 and shape["grp"] == 2 and shape["ch"] == 2 and shape["sub"] == 2


def solution(mesh):
    return jax.shard_map(
        fast_shards if fits(mesh) else shards,
        mesh=mesh,
        in_specs=(
            P(("grp", "seq")),
            P(("grp", "seq"), ("ch", "sub")),
            P(None, ("ch", "sub")),
            P("seq", None, ("ch", "sub")),
            P(None, None, ("ch", "sub")),
            P(None, ("ch", "sub")),
            P(None, ("ch", "sub")),
            P(("ch", "sub")),
        ),
        out_specs=P(("grp", "seq"), ("ch", "sub")),
        check_vma=False,
    )
```

time: 116 us -> 100 us (0.86)
  the two profiles are of different devices: /device:TPU:6 before, /device:TPU:0 now
where the time goes in v1:
time: 100 us
  Pallas kernels  95 us (95%)
  local copies, waits for them, and re-layouts  2.89 us (3%)
  matrix products  2.33 us (2%)
    pallas_call x1, Pallas kernels, fused(): pl.pallas_call(fused_block, out_shape=jax.ShapeDtypeStruct((rows, channel...  95 us
    unnamed x3, local copies, waits for them, and re-layouts  2.89 us
    dot_general x1, matrix products, fast_shards(): embedded = jnp.dot(onehot, embedding, preferred_element_type=jnp.float32)  2.33 us

profile of v1, /device:TPU:0, one launch (start us, length us, event | category | flops | bytes accessed | tf_op | source)
XLA Modules:
  0.0 100.2 jit_solution(9379480442382064085)
XLA Ops:
  0.0 0.0 copy-start
  0.0 1.2 %copy-done = bf16[512,1024]{1,0:T(8,128)(2,1)S(1)} copy-done((bf16[512,1024]{1,0:T(8,128)(2,1)S(1)}, bf16[512,1024]{1,0:T(8,128)(2,1)}, u32[]{:S(2)}) %copy-start) | copy-done | bytes 1048600
  1.2 2.3 %fusion.x_ref = bf16[256,1024]{1,0:T(8,128)(2,1)} fusion(bf16[512,1024]{1,0:T(8,128)(2,1)S(1)} %copy-done, bf16[256,1024]{1,0:T(8,128)(2,1)} %param.9, s32[256]{0:T(256)} %param.8), kind=kOutput, calls=%fused_computation.1 | convolution fusion | flops 269352960 | bytes 2098176 | tf_op jit(solution)/shard_map/dot_general | solution.py:707
  3.6 95.0 %shard_map.82 = bf16[256,512]{1,0:T(8,128)(2,1)} custom-call(bf16[256,1024]{1,0:T(8,128)(2,1)} %fusion.x_ref, bf16[3,1024,512]{2,1,0:T(8,128)(2,1)} %bitcast.3, f32[3,3,512]{2,1,0:T(4,128)} %taps_ref.1, f32[16,512]{1,0:T(8,128)} %rate_ref.1, f32[16,512]{1,0:T(8,128)} %residue_ref.1, f32[1,512]{1,0:T(1,128)} %bitcast.4), custom_call_target="tpu_custom_call" | custom-call | tf_op jit(solution)/shard_map/pallas_call | solution.py:663
  98.6 1.7 %copy.10 = bf16[256,512]{1,0:T(8,128)(2,1)} copy(bf16[256,512]{1,0:T(8,128)(2,1)} %shard_map.82) | data formatting | bytes 524288
Async XLA Ops:
  0.0 1.2 %copy-start = (bf16[512,1024]{1,0:T(8,128)(2,1)S(1)}, bf16[512,1024]{1,0:T(8,128)(2,1)}, u32[]{:S(2)}) copy-start(bf16[512,1024]{1,0:T(8,128)(2,1)} %param.10) | copy-start | bytes 3145732

commit v2 on v1

--- a/solution.py
+++ b/solution.py
@@ -163,15 +163,18 @@
 
 
 MESH = pl.DeviceIdType.MESH
-PIECES = 4
-AHEAD = 3
+PIECES = 8
+AHEAD = 2
+RELAY = 3
+BEHIND = 3
+EARLY = 2
 SEGMENTS = 8
 
 
 def fused_block(
-    x_ref, w_ref, taps_ref, rate_ref, residue_ref, skip_ref, out_ref,
-    held, weights, stage, outbox, inbox, edge, halo, proj, values, conv, enter, ends, states,
-    load_sem, wide_send, wide_recv, weight_send, weight_recv, x_send, x_recv, via_send, via_recv,
+    ids_ref, residual_ref, table_ref, w_ref, taps_ref, rate_ref, residue_ref, skip_ref, out_ref,
+    x_ref, residual, table, held, weights, stage, outbox, inbox, edge, halo, proj, values, conv, enter, ends, states,
+    in_sem, load_sem, wide_send, wide_recv, weight_send, weight_recv, x_send, x_recv, via_send, via_recv,
     box_send, box_recv, edge_send, edge_recv, end_send, end_recv,
 ):
     y = lax.axis_index("grp")
@@ -219,7 +222,23 @@
     def loaded(u):
         pltpu.make_async_copy(w_ref.at[0, :, pl.ds(0, lanes)], weights.at[mine, u], load_sem.at[u]).wait()
 
-    for u in range(units):
+    fetch = [
+        pltpu.make_async_copy(table_ref, table, in_sem.at[0]),
+        pltpu.make_async_copy(residual_ref, residual, in_sem.at[1]),
+    ]
+
+    @pl.when(is_outer)
+    def _():
+        load(0).start()
+
+    for copy in fetch:
+        copy.start()
+
+    @pl.when(is_inner)
+    def _():
+        load(0).start()
+
+    for u in range(1, units):
         load(u).start()
     halo[...] = jnp.zeros_like(halo)
     states[...] = jnp.zeros_like(states)
@@ -246,6 +265,14 @@
         remote(at, at, weight_send.at[u], weight_recv.at[u], other_group).wait_recv()
         weight_wide(u).start()
 
+    def prepare():
+        for copy in fetch:
+            copy.wait()
+        vocab = lax.broadcasted_iota(jnp.int32, (table.shape[0], rows), 0)
+        onehot = (vocab == ids_ref[...]).astype(f32).astype(bf16)
+        embedded = lax.dot_general(onehot, table[...], (((0,), (0,)), ((), ())), preferred_element_type=f32)
+        x_ref[...] = (residual[...].astype(f32) + embedded).astype(bf16)
+
     step = rows // PIECES
     direct = PIECES // 2
 
@@ -279,23 +306,33 @@
             {"seq": relay_goal},
         )
 
-    def send_via():
+    def own_sibling(p):
+        return remote(
+            x_ref.at[piece(p)], held.at[z, sub, piece(p)], x_send.at[1 + parts + z, p], x_recv.at[z, sub, p], sibling
+        )
+
+    def own_first():
+        @pl.when(stays)
+        def _():
+            for p in range(direct):
+                own_across(p).start()
+            for p in range(PIECES):
+                own_local(p).start()
+                own_sibling(p).start()
+
+    def own_rest():
         @pl.when(stays)
         def _():
             for p in range(direct, PIECES):
                 own_across(p).start()
 
+    def send_via():
         @pl.when(jnp.logical_not(stays))
         def _():
             for p in range(direct, PIECES):
                 own_via(p).start()
 
     def send_direct():
-        @pl.when(stays)
-        def _():
-            for p in range(direct):
-                own_local(p).start()
-
         @pl.when(jnp.logical_not(stays))
         def _():
             for p in range(direct):
@@ -336,6 +373,14 @@
             p = second + n
             arrived(t, sub, p)
             to_sibling(t, p).start()
+
+    def own_block():
+        for p in range(PIECES):
+            arrived(z, sub, p)
+
+            @pl.when(jnp.logical_not(at_home))
+            def _():
+                to_sibling(z, p).start()
 
     def from_sibling(t):
         for p in range(PIECES):
@@ -486,22 +531,22 @@
 
     @pl.when(is_outer)
     def _():
-        loaded(0)
-        weight_up(0).start()
-        send_via()
-        send_direct()
-        for u in range(1, AHEAD):
+        for u in range(EARLY):
             loaded(u)
             weight_up(u).start()
+        prepare()
+        send_via()
+        own_first()
+        own_rest()
+        send_direct()
         send_relay()
-        for u in range(AHEAD, units):
+        for u in range(EARLY, units):
             loaded(u)
             weight_up(u).start()
 
         @pl.when(sub == mine)
         def _():
-            primary(z)
-            secondary(z)
+            own_block()
 
         @pl.when(sub != mine)
         def _():
@@ -524,7 +569,9 @@
     @pl.when(is_inner)
     def _():
         handles_near = sub == mine
+        prepare()
         send_via()
+        own_first()
         send_direct()
         send_relay()
         weight_share(0)
@@ -532,7 +579,7 @@
         weight_share(1)
         secondary(far_near)
         primary(far_outer)
-        for u in range(2, AHEAD):
+        for u in range(2, AHEAD + RELAY - 1):
             weight_share(u)
         from_sibling(far_near)
 
@@ -542,15 +589,15 @@
             far(0, far_near, u)
 
         secondary(far_outer)
-        primary(z)
-        weight_share(AHEAD)
+        own_rest()
+        weight_share(AHEAD + RELAY - 1)
 
         @pl.when(handles_near)
         def _():
             primary(outer)
 
         from_sibling(far_outer)
-        lag = 3
+        lag = BEHIND + 2
 
         @pl.loop(0, units + lag)
         def _(i):
@@ -563,13 +610,13 @@
                 weights_ready(i + AHEAD)
                 far(0, far_near, i + AHEAD)
 
-            @pl.when(i + AHEAD + 1 < units)
-            def _():
-                weight_share(i + AHEAD + 1)
-
-            @pl.when(i == 0)
-            def _():
-                secondary(z)
+            @pl.when(i + AHEAD + RELAY < units)
+            def _():
+                weight_share(i + AHEAD + RELAY)
+
+            @pl.when(i == BEHIND - 1)
+            def _():
+                own_block()
 
                 @pl.when(handles_near)
                 def _():
@@ -581,10 +628,10 @@
                 def _():
                     from_sibling(outer)
 
-            @pl.when((i > 0) & (i <= units))
-            def _():
-                to_outer(i - 1)
-                finished(both(z, i - 1), i - 1)
+            @pl.when((i >= BEHIND) & (i < units + BEHIND))
+            def _():
+                to_outer(i - BEHIND)
+                finished(both(z, i - BEHIND), i - BEHIND)
 
             @pl.when((i >= pairs + lag - 1) & (i < units + lag - 1))
             def _():
@@ -595,14 +642,16 @@
                 mix(i - lag)
 
     for p in range(PIECES):
-        @pl.when(jnp.logical_not(stays) | (p >= direct))
-        def _():
-            own_direct(p).wait_send()
+        own_direct(p).wait_send()
 
     @pl.when(jnp.logical_not(relay_stays))
     def _():
         for p in range(direct, PIECES):
             relay(p).wait_send()
+
+    def own_sent():
+        for p in range(PIECES):
+            to_sibling(z, p).wait_send()
 
     def sent(t):
         for n in range(direct):
@@ -612,13 +661,13 @@
 
     @pl.when(is_outer & (sub == mine))
     def _():
-        sent(z)
+        own_sent()
 
     @pl.when(is_inner)
     def _():
         sent(far_near)
         sent(far_outer)
-        sent(z)
+        own_sent()
 
         @pl.when(sub == mine)
         def _():
@@ -649,8 +698,8 @@
                 ).wait_send()
 
 
-def fused(inputs, weight, short_filter, decay_rate, residue, skip):
-    rows, width = inputs.shape
+def fused(token_ids, residual_in, embedding, weight, short_filter, decay_rate, residue, skip):
+    rows, width = residual_in.shape
     groups, _, channels = weight.shape
     parts = 4
     modes = decay_rate.shape[0]
@@ -662,10 +711,13 @@
     vmem = pl.BlockSpec(memory_space=pltpu.VMEM)
     return pl.pallas_call(
         fused_block,
-        out_shape=jax.ShapeDtypeStruct((rows, channels), jnp.bfloat16),
-        in_specs=[vmem, pl.BlockSpec(memory_space=pl.ANY)] + [vmem] * 4,
+        out_shape=jax.ShapeDtypeStruct((rows, channels), f32),
+        in_specs=[vmem] + [pl.BlockSpec(memory_space=pl.ANY)] * 3 + [vmem] * 4,
         out_specs=vmem,
         scratch_shapes=[
+            pltpu.VMEM((rows, width), bf16),
+            pltpu.VMEM((rows, width), bf16),
+            pltpu.VMEM(embedding.shape, bf16),
             pltpu.VMEM((parts, 2, rows, width), bf16),
             pltpu.VMEM((2, units, width, lanes), bf16),
             pltpu.VMEM((PIECES - PIECES // 2, rows // PIECES, width), bf16),
@@ -679,6 +731,7 @@
             pltpu.VMEM((blocks, modes, SEGMENTS, lanes), f32),
             pltpu.VMEM((blocks, modes, lanes), f32),
             pltpu.VMEM((parts - 1, blocks, modes, lanes), f32),
+            dma((2,)),
             dma((units,)),
             dma((units,)),
             dma((units,)),
@@ -698,15 +751,13 @@
         compiler_params=pltpu.CompilerParams(
             collective_id=0, has_side_effects=True, vmem_limit_bytes=60 * 2**20
         ),
-    )(inputs, weight, short_filter, decay_rate, residue, skip.reshape(1, -1))
+    )(token_ids.reshape(1, -1), residual_in, embedding, weight, short_filter, decay_rate, residue, skip.reshape(1, -1))
 
 
 def fast_shards(token_ids, residual_in, embedding, in_weight, short_filter, decay_rate, residue, skip):
-    vocab_size = embedding.shape[0]
-    onehot = (token_ids[:, None] == jnp.arange(vocab_size, dtype=jnp.int32)[None, :]).astype(jnp.bfloat16)
-    embedded = jnp.dot(onehot, embedding, preferred_element_type=jnp.float32)
-    inputs = (residual_in.astype(jnp.float32) + embedded).astype(jnp.bfloat16)
-    return fused(inputs, in_weight.transpose(1, 0, 2), short_filter, decay_rate, residue, skip)
+    weight = in_weight.transpose(1, 0, 2)
+    mixed = fused(token_ids, residual_in, embedding, weight, short_filter, decay_rate, residue, skip)
+    return mixed.astype(jnp.bfloat16)
 
 
 def fits(mesh):

time: 100 us -> 79.3 us (0.79)
  Pallas kernels: 95 us -> 77.3 us
  local copies, waits for them, and re-layouts: 2.89 us -> 0 us
  matrix products: 2.33 us -> 0 us
  other arithmetic: 0 us -> 1.78 us
    pallas_call x1, Pallas kernels: 95 us -> 77.3 us  [fused(): pl.pallas_call(fused_block, out_shape=jax.ShapeDtypeStruct((rows, channel...]
    unnamed x3 -> x0, local copies, waits for them, and re-layouts: 2.89 us -> none
    dot_general x1 -> x0, matrix products: 2.33 us -> none  [fast_shards(): embedded = jnp.dot(onehot, embedding, preferred_element_type=jnp.float32)]
    convert_element_type x0 -> x1, other arithmetic: none -> 1.78 us  [fast_shards(): return mixed.astype(jnp.bfloat16)]
where the time goes in v2:
time: 79.3 us; the launch traced here: 79.1 us
  Pallas kernels  77.3 us (97%)
  other arithmetic  1.78 us (2%)
    pallas_call x1, Pallas kernels, fused(): pl.pallas_call(fused_block, out_shape=jax.ShapeDtypeStruct((rows, channel...  77.3 us
    convert_element_type x1, other arithmetic, fast_shards(): return mixed.astype(jnp.bfloat16)  1.78 us

profile of v2, /device:TPU:0, one launch (start us, length us, event | category | flops | bytes accessed | tf_op | source)
XLA Modules:
  0.0 79.1 jit_solution(13745446554969910285)
XLA Ops:
  0.0 77.3 %shard_map.82 = f32[256,512]{1,0:T(8,128)} custom-call(s32[1,256]{1,0:T(1,128)} %bitcast.5, bf16[256,1024]{1,0:T(8,128)(2,1)} %residual_ref.1, bf16[512,1024]{1,0:T(8,128)(2,1)} %table_ref.1, bf16[3,1024,512]{2,1,0:T(8,128)(2,1)} %bitcast.3, f32[3,3,512]{2,1,0:T(4,128)} %taps_ref.1, f32[16,512]{1,0:T(8,128)} %rate_ref.1, f32[16,512]{1,0:T(8,128)} %residue_ref.1, ...), custom_call_target="tpu_custom_call" | custom-call | tf_op jit(solution)/shard_map/pallas_call | solution.py:712
  77.3 1.8 %convert_element_type.3 = bf16[256,512]{1,0:T(8,128)(2,1)} convert(f32[256,512]{1,0:T(8,128)} %shard_map.82) | non-fusion elementwise | flops 131072 | bytes 786432 | tf_op jit(solution)/shard_map/convert_element_type | solution.py:760
